TPU v7x, 512 devices: a whole 4x8x8 slice. The times are simulated.
512 devices in a mesh: ex: 64 (over y, z_hi, core), feat: 8 (over x, z_lo).
Axes of the slice: x: 4, y: 8, z: 8 (z_hi: 4, z_lo: 2; z = z_hi * 2 + z_lo), core: 2. Of those that a mesh axis runs over, the one named last changes fastest.
Arguments:
- proj_inputs: bfloat16 [2, 2048, 24, 2048], P(None, 'ex', None, 'feat'), may hold values from -6 to 6
- out_cotangent: bfloat16 [2, 2048, 24, 4096], P(None, 'ex', None, 'feat'), may hold values from -200 to 200
- seq_lengths: int32 [2048], P('ex'), may hold values from 6 to 24, as said below
- frozen_adapter: bfloat16 [2, 128, 2048], P(None, None, 'feat'), may hold values from -0.125 to 0.125
- left_factor: bfloat16 [2, 512, 4096], P(None, None, 'feat'), may hold values from -0.09375 to 0.09375
- right_factor: bfloat16 [2, 128, 16], replicated, may hold values from -0.5 to 0.5
- valid_grads: bfloat16 [256, 8192], P('ex', 'feat'), may hold values from -200 to 200
Outputs:
- scores: float32 [2048, 256], P('ex')
Inputs may be any that keep to these rules, and one draw needn't show every extreme that they name: Tokens at positions below seq_lengths are live; in every aligned block of 32 examples one example has all 24 tokens live and one has the fewest allowed.
All inputs are finite; a program needn't handle non-finite values.
Results may differ from a plain program's by a relative error of at most 0.0037.
Values may be sent and summed in bfloat16 or wider, within the bound.
No kernel may reach another device: no remote copies, remote signals or barrier semaphores. Data moves between devices by JAX's collectives and lax.ppermute only.
A program may use at most 64 MiB of HBM per device.

v0:
```python
import math
import jax
import jax.numpy as jnp
from jax import lax
from jax.sharding import PartitionSpec as P


def body(
    proj_inputs, out_cotangent, seq_lengths, frozen_adapter, left_factor, right_factor, valid_grads
):
    highest = lax.Precision.HIGHEST
    layer_count, example_count, token_count, _ = proj_inputs.shape
    feat_count = lax.axis_size("feat")
    proj_count = right_factor.shape[2]
    owned_rows = left_factor.shape[1] // feat_count
    position = jnp.arange(token_count, dtype=jnp.int32)
    live_tokens = (position[None, :] < seq_lengths[:, None]).astype(jnp.float32)
    adapted = jnp.einsum(
        "lesh,lrh->lesr", proj_inputs, frozen_adapter, preferred_element_type=jnp.float32
    )
    right_wide = right_factor.astype(jnp.float32)
    adapted = lax.psum(adapted, "feat")
    right_rows = jnp.einsum("lesr,lrb->lesb", adapted, right_wide, precision=highest)
    right_rows = (right_rows * live_tokens[None, :, :, None]).astype(jnp.bfloat16)
    flat_cotan = out_cotangent.reshape(
        layer_count, example_count * token_count, out_cotangent.shape[3]
    )
    term = jnp.einsum("lkd,ltd->klt", left_factor, flat_cotan, preferred_element_type=jnp.float32)
    left_rows = lax.psum_scatter(
        term.reshape(lax.axis_size("feat") * owned_rows, layer_count * example_count * token_count),
        "feat",
        scatter_dimension=0,
        tiled=True,
    )
    own_rows = left_rows.shape[0]
    left_rows = left_rows.reshape(own_rows, layer_count, example_count, token_count)
    projected = jnp.einsum(
        "kles,lesb->ekb", left_rows, right_rows.astype(jnp.float32), precision=highest
    )
    projected = projected.reshape(example_count, own_rows * proj_count)
    train_squares = jnp.sum(projected * projected, axis=1)
    rounded = projected.astype(jnp.bfloat16)
    scaling = math.sqrt(valid_grads.shape[1] * feat_count)
    valid_wide = valid_grads.astype(jnp.float32)
    valid_squares = jnp.sum(valid_wide * valid_wide, axis=1)
    products = jnp.einsum(
        "ek,vk->ev",
        lax.all_gather(rounded, "ex", axis=0, tiled=True),
        valid_grads,
        preferred_element_type=jnp.float32,
    )
    products, valid_squares, train_squares = lax.psum(
        (products, valid_squares, train_squares), "feat"
    )
    products = products / jnp.sqrt(valid_squares + 1e-06)[None, :]
    products = lax.all_to_all(products, "ex", split_axis=0, concat_axis=1, tiled=True)
    return scaling * products / jnp.sqrt(train_squares + 1e-06)[:, None]


def solution(mesh):
    return jax.shard_map(
        body,
        mesh=mesh,
        in_specs=(
            P(None, "ex", None, "feat"),
            P(None, "ex", None, "feat"),
            P("ex"),
            P(None, None, "feat"),
            P(None, None, "feat"),
            P(),
            P("ex", "feat"),
        ),
        out_specs=P("ex", None),
        check_vma=False,
    )
```

profile of v0, /device:TPU:1, one launch (start us, length us, event | category | flops | bytes accessed | tf_op | source)
XLA Modules:
  0.0 342.0 jit_solution(11740228024214441054)
XLA Ops:
  6.5 0.0 copy-start
  6.5 0.0 copy-start.1
  6.5 0.0 all-reduce.3.cloned.1.call-start
  6.5 2.5 fusion.3
  9.1 0.0 all-reduce.3.cloned.1.call-update
  9.1 0.0 reduce-scatter.4.cloned.1.call-start
  9.1 0.0 copy-done
  9.2 0.0 copy-done.1
  9.2 2.7 fusion.7
  11.9 3.5 %copy.20 = f32[512,1536]{1,0:T(8,128)} copy(f32[512,1536]{0,1:T(8,128)} %bitcast.34) | data formatting | bytes 6291456
  15.4 0.0 copy-start.4
  15.4 0.0 copy-start.3
  15.4 0.0 copy-start.2
  15.4 0.0 reduce-scatter.4.cloned.1.call-update
  15.5 0.0 all-gather.2.cloned.1.call-start
  15.5 0.6 copy-done.4
  16.1 0.1 fusion.5
  16.2 83.7 %all-reduce.3.cloned.1.call-done = f32[2,32,24,128]{3,2,1,0:T(8,128)} async-done(((f32[2,32,24,128]{3,2,1,0:T(8,128)}), f32[2,32,24,128]{3,2,1,0:T(8,128)}) %all-reduce.3.cloned.1.call-update) | async-done | bytes 786448 | tf_op jit(solution)/shard_map/psum | solution.py:22
  99.8 0.0 copy-done.3
  99.8 3.2 fusion
  103.0 80.2 %reduce-scatter.4.cloned.1.call-done = f32[64,1536]{1,0:T(8,128)} async-done(((f32[512,1536]{1,0:T(8,128)}), f32[64,1536]{1,0:T(8,128)}) %reduce-scatter.4.cloned.1.call-update) | async-done | bytes 393232
  183.2 1.3 copy.21
  184.5 0.8 multiply_reduce_fusion
  185.3 0.3 copy.15
  185.6 0.8 copy.16
  186.3 0.0 all-gather.2.cloned.1.call-update
  186.3 0.0 copy-done.2
  186.4 0.1 multiply_reduce_fusion.1
  186.5 88.7 %all-gather.2.cloned.1.call-done = bf16[2048,1024]{1,0:T(8,128)(2,1)} async-done(((bf16[32,1024]{1,0:T(8,128)(2,1)}), bf16[2048,1024]{1,0:T(8,128)(2,1)}) %all-gather.2.cloned.1.call-update) | async-done | bytes 4194320 | tf_op jit(solution)/shard_map/all_gather | solution.py:48
  275.2 3.4 fusion.8
  278.6 28.1 %all-reduce = (f32[2048,4]{0,1:T(4,128)S(1)}, f32[4]{0:T(128)S(1)}, f32[32]{0:T(128)S(1)}) all-reduce(f32[2048,4]{0,1:T(4,128)S(1)} %fusion.8, f32[4]{0:T(128)S(1)} %multiply_reduce_fusion.1, f32[32]{0:T(128)S(1)} %get-tuple-element.8), channel_id=1, replica_groups=mesh['ex'=64,'feat'=8] {'feat'}, use_global_device_ids=true, to_apply=%region_2.0 | all-reduce | flops 8228 | bytes 65824 | tf_op jit(solution)/shard_map/psum | solution.py:52
  306.7 0.1 broadcast_divide_fusion.1
  306.7 0.1 all_to_all.10
  306.8 0.1 copy.29
  306.9 0.8 reshape.48
  307.7 13.9 %all-to-all-start = ((f32[64,1,128]{2,1,0:T(1,128)}), f32[64,1,128]{2,1,0:T(1,128)S(1)}, u32[]{:S(2)}, u32[]{:S(2)}) async-start(f32[64,1,128]{2,1,0:T(1,128)} %reshape.48), calls=%async_computation | async-start | bytes 65536 | tf_op jit(solution)/shard_map/all_to_all | solution.py:56
  321.7 11.7 %all-to-all-done = f32[64,1,128]{2,1,0:T(1,128)S(1)} async-done(((f32[64,1,128]{2,1,0:T(1,128)}), f32[64,1,128]{2,1,0:T(1,128)S(1)}, u32[]{:S(2)}, u32[]{:S(2)}) %all-to-all-start) | async-done | bytes 32800 | tf_op jit(solution)/shard_map/all_to_all | solution.py:56
  333.4 0.5 broadcast.25
  333.9 0.7 reduce.1
  334.6 0.1 reshape.49
  334.8 0.7 copy.18
  (4 shorter events, 0.1 us)
Async XLA Ops:
  6.5 2.6 copy-start
  6.5 2.6 copy-start.1
  6.5 93.3 %all-reduce.3.cloned.1.call-start = ((), (), s32[]{:S(2)}) async-start(), calls=%async_computation.2 | async-start | bytes 1572864 | tf_op jit(solution)/shard_map/psum | solution.py:22
  9.1 174.1 %reduce-scatter.4.cloned.1.call-start = ((), (), s32[]{:S(2)}) async-start(), calls=%async_computation.4 | async-start | bytes 3538944
  15.4 0.7 copy-start.4
  15.4 84.4 %copy-start.3 = (bf16[2,128,16]{1,2,0:T(8,128)(2,1)S(1)}, bf16[2,128,16]{1,2,0:T(8,128)(2,1)}, u32[]{:S(2)}) copy-start(bf16[2,128,16]{1,2,0:T(8,128)(2,1)} %param.12) | copy-start | bytes 24580
  15.4 170.9 %copy-start.2 = (bf16[4,1024]{1,0:T(4,128)(2,1)S(1)}, bf16[4,1024]{1,0:T(4,128)(2,1)}, u32[]{:S(2)}) copy-start(bf16[4,1024]{1,0:T(4,128)(2,1)} %param.13) | copy-start | bytes 24580
  15.5 259.8 %all-gather.2.cloned.1.call-start = ((), (), s32[]{:S(2)}) async-start(), calls=%async_computation.3 | async-start | bytes 4259840 | tf_op jit(solution)/shard_map/all_gather | solution.py:48
  307.7 25.7 %all-to-all-start = ((f32[64,1,128]{2,1,0:T(1,128)}), f32[64,1,128]{2,1,0:T(1,128)S(1)}, u32[]{:S(2)}, u32[]{:S(2)}) async-start(f32[64,1,128]{2,1,0:T(1,128)} %reshape.48), calls=%async_computation | async-start | bytes 65536 | tf_op jit(solution)/shard_map/all_to_all | solution.py:56
Sparse Core Ops, SparseCore 0:
  10.3 89.4 all-reduce.2
  102.7 80.5 reduce-scatter.3
  186.5 88.6 all-gather.1
where the time goes:
time: 342 us
  waiting for transfers between devices  264 us (77%)
  blocking collectives  28.1 us (8%)
  starting transfers between devices  14 us (4%)
  between operations  13.2 us (4%)
  matrix products  12.6 us (4%)
  local copies, waits for them, and re-layouts  8.7 us (3%)
    all_gather x1, waiting for transfers between devices, body(): lax.all_gather(rounded, 'ex', axis=0, tiled=True)  88.7 us
    psum x1, waiting for transfers between devices, body(): adapted = lax.psum(adapted, 'feat')  83.7 us
    unnamed x4, waiting for transfers between devices  80.3 us
    psum x1, blocking collectives, body(): lax.psum((products, valid_squares, train_squares), 'feat')  28.1 us
    all_to_all x1, starting transfers between devices, body(): lax.all_to_all(products, 'ex', split_axis=0, concat_axis=1, tiled=True)  13.9 us
    all_to_all x1, waiting for transfers between devices, body(): lax.all_to_all(products, 'ex', split_axis=0, concat_axis=1, tiled=True)  11.7 us
  transfers between devices with their start and end apart: 4, of which 4 were waited for; matrix products, arithmetic and copies ran while one was open for 3% of the time, Pallas kernels for 0%

commit v1 on v0

--- a/solution.py
+++ b/solution.py
@@ -19,7 +19,7 @@
         "lesh,lrh->lesr", proj_inputs, frozen_adapter, preferred_element_type=jnp.float32
     )
     right_wide = right_factor.astype(jnp.float32)
-    adapted = lax.psum(adapted, "feat")
+    adapted = jnp.sum(lax.all_gather(adapted, "feat"), axis=0)
     right_rows = jnp.einsum("lesr,lrb->lesb", adapted, right_wide, precision=highest)
     right_rows = (right_rows * live_tokens[None, :, :, None]).astype(jnp.bfloat16)
     flat_cotan = out_cotangent.reshape(

time: 342 us -> 399 us (1.17)
  waiting for transfers between devices: 264 us -> 317 us
    all_gather x0 -> x1, waiting for transfers between devices: none -> 135 us  [body(): adapted = jnp.sum(lax.all_gather(adapted, 'feat'), axis=0)]
    psum x1 -> x0, waiting for transfers between devices: 83.7 us -> none  [body(): adapted = lax.psum(adapted, 'feat')]
    unnamed x14 -> x16, local copies, waits for them, and re-layouts: 6.26 us -> 8.19 us
  transfers between devices with their start and end apart: 4 -> 4, of which waited for: 4 -> 4; matrix products, arithmetic and copies ran while one was open for 3% -> 1% of each run, Pallas kernels for 0% -> 0%
where the time goes in v1:
time: 399 us; the launch traced here: 398 us
  waiting for transfers between devices  317 us (79%)
  blocking collectives  28.1 us (7%)
  starting transfers between devices  14 us (4%)
  between operations  13.2 us (3%)
  matrix products  11.3 us (3%)
  local copies, waits for them, and re-layouts  10.6 us (3%)
  other arithmetic  4.24 us (1%)
    all_gather x1, waiting for transfers between devices, body(): adapted = jnp.sum(lax.all_gather(adapted, 'feat'), axis=0)  135 us
    all_gather x1, waiting for transfers between devices, body(): lax.all_gather(rounded, 'ex', axis=0, tiled=True)  89.8 us
    unnamed x4, waiting for transfers between devices  80.2 us
    psum x1, blocking collectives, body(): lax.psum((products, valid_squares, train_squares), 'feat')  28.1 us
    all_to_all x1, starting transfers between devices, body(): lax.all_to_all(products, 'ex', split_axis=0, concat_axis=1, tiled=True)  13.9 us
    all_to_all x1, waiting for transfers between devices, body(): lax.all_to_all(products, 'ex', split_axis=0, concat_axis=1, tiled=True)  11.7 us
    unnamed x16, local copies, waits for them, and re-layouts  8.19 us
  transfers between devices with their start and end apart: 4, of which 4 were waited for; matrix products, arithmetic and copies ran while one was open for 1% of the time, Pallas kernels for 0%

profile of v1, /device:TPU:1, one launch (start us, length us, event | category | flops | bytes accessed | tf_op | source)
XLA Modules:
  0.0 398.2 jit_solution(14142326388233238354)
XLA Ops:
  6.5 0.0 copy-start
  6.5 0.0 reduce-scatter.4.cloned.1.call-start
  6.5 1.4 copy-done
  7.9 3.9 fusion.7
  11.8 3.6 copy.25
  15.4 0.0 copy-start.1
  15.4 0.0 copy-start.2
  15.4 0.0 copy-start.5
  15.4 0.0 reduce-scatter.4.cloned.1.call-update
  15.4 0.0 all-gather.6.cloned.1.call-start
  15.5 1.1 copy-done.1
  16.6 0.0 copy-done.2
  16.6 1.3 fusion.3
  17.8 0.0 all-gather.6.cloned.1.call-update
  17.8 0.0 all-gather.4.cloned.1.call-start
  17.9 0.0 copy-done.5
  17.9 0.1 fusion.5
  18.0 80.2 %reduce-scatter.4.cloned.1.call-done = f32[64,1536]{1,0:T(8,128)} async-done(((f32[512,1536]{1,0:T(8,128)}), f32[64,1536]{1,0:T(8,128)}) %reduce-scatter.4.cloned.1.call-update) | async-done | bytes 393232
  98.1 1.3 copy.26
  99.4 135.0 %all-gather.6.cloned.1.call-done = f32[16,32,24,128]{3,2,1,0:T(8,128)} async-done(((f32[2,32,24,128]{3,2,1,0:T(8,128)}), f32[16,32,24,128]{3,2,1,0:T(8,128)}) %all-gather.6.cloned.1.call-update) | async-done | bytes 6291472 | tf_op jit(solution)/shard_map/all_gather | solution.py:22
  234.4 0.0 copy-start.4
  234.4 0.0 copy-start.3
  234.4 3.2 reduce_sum.27
  237.6 0.0 copy-done.4
  237.6 2.1 fusion
  239.7 0.8 multiply_reduce_fusion
  240.5 0.3 copy.20
  240.8 0.8 copy.21
  241.5 0.0 all-gather.4.cloned.1.call-update
  241.5 0.0 copy-done.3
  241.5 0.1 multiply_reduce_fusion.1
  241.7 89.8 %all-gather.4.cloned.1.call-done = bf16[2048,1024]{1,0:T(8,128)(2,1)} async-done(((bf16[32,1024]{1,0:T(8,128)(2,1)}), bf16[2048,1024]{1,0:T(8,128)(2,1)}) %all-gather.4.cloned.1.call-update) | async-done | bytes 4194320 | tf_op jit(solution)/shard_map/all_gather | solution.py:48
  331.4 3.4 fusion.8
  334.8 28.1 %all-reduce = (f32[2048,4]{0,1:T(4,128)S(1)}, f32[4]{0:T(128)S(1)}, f32[32]{0:T(128)S(1)}) all-reduce(f32[2048,4]{0,1:T(4,128)S(1)} %fusion.8, f32[4]{0:T(128)S(1)} %multiply_reduce_fusion.1, f32[32]{0:T(128)S(1)} %get-tuple-element.8), channel_id=1, replica_groups=mesh['ex'=64,'feat'=8] {'feat'}, use_global_device_ids=true, to_apply=%region_2.0 | all-reduce | flops 8228 | bytes 65824 | tf_op jit(solution)/shard_map/psum | solution.py:52
  362.9 0.1 broadcast_divide_fusion.1
  363.0 0.1 all_to_all.10
  363.1 0.1 copy.34
  363.2 0.8 reshape.49
  363.9 13.9 %all-to-all-start = ((f32[64,1,128]{2,1,0:T(1,128)}), f32[64,1,128]{2,1,0:T(1,128)S(1)}, u32[]{:S(2)}, u32[]{:S(2)}) async-start(f32[64,1,128]{2,1,0:T(1,128)} %reshape.49), calls=%async_computation | async-start | bytes 65536 | tf_op jit(solution)/shard_map/all_to_all | solution.py:56
  377.9 11.7 %all-to-all-done = f32[64,1,128]{2,1,0:T(1,128)S(1)} async-done(((f32[64,1,128]{2,1,0:T(1,128)}), f32[64,1,128]{2,1,0:T(1,128)S(1)}, u32[]{:S(2)}, u32[]{:S(2)}) %all-to-all-start) | async-done | bytes 32800 | tf_op jit(solution)/shard_map/all_to_all | solution.py:56
  389.6 0.5 broadcast.25
  390.1 0.7 reduce.1
  390.8 0.1 reshape.50
  391.0 0.7 copy.23
  (4 shorter events, 0.1 us)
Async XLA Ops:
  6.5 1.4 copy-start
  6.5 91.6 %reduce-scatter.4.cloned.1.call-start = ((), (), s32[]{:S(2)}) async-start(), calls=%async_computation.4 | async-start | bytes 3538944
  15.4 1.1 copy-start.1
  15.4 1.1 copy-start.2
  15.4 2.5 copy-start.5
  15.4 219.0 %all-gather.6.cloned.1.call-start = ((), (), s32[]{:S(2)}) async-start(), calls=%async_computation.3 | async-start | bytes 7077888 | tf_op jit(solution)/shard_map/all_gather | solution.py:22
  17.8 313.6 %all-gather.4.cloned.1.call-start = ((), (), s32[]{:S(2)}) async-start(), calls=%async_computation.2 | async-start | bytes 4259840 | tf_op jit(solution)/shard_map/all_gather | solution.py:48
  234.4 3.2 copy-start.4
  234.4 7.1 %copy-start.3 = (bf16[4,1024]{1,0:T(4,128)(2,1)S(1)}, bf16[4,1024]{1,0:T(4,128)(2,1)}, u32[]{:S(2)}) copy-start(bf16[4,1024]{1,0:T(4,128)(2,1)} %param.13) | copy-start | bytes 24580
  363.9 25.7 %all-to-all-start = ((f32[64,1,128]{2,1,0:T(1,128)}), f32[64,1,128]{2,1,0:T(1,128)S(1)}, u32[]{:S(2)}, u32[]{:S(2)}) async-start(f32[64,1,128]{2,1,0:T(1,128)} %reshape.49), calls=%async_computation | async-start | bytes 65536 | tf_op jit(solution)/shard_map/all_to_all | solution.py:56
Sparse Core Ops, SparseCore 0:
  15.6 82.5 reduce-scatter.3
  100.2 134.1 all-gather.5
  241.7 89.7 all-gather.3

commit v2 on v0

--- a/solution.py
+++ b/solution.py
@@ -45,7 +45,9 @@
     valid_squares = jnp.sum(valid_wide * valid_wide, axis=1)
     products = jnp.einsum(
         "ek,vk->ev",
-        lax.all_gather(rounded, "ex", axis=0, tiled=True),
+        jnp.concatenate(
+            lax.all_to_all(jnp.stack([rounded] * lax.axis_size("ex")), "ex", 0, 0), axis=0
+        ),
         valid_grads,
         preferred_element_type=jnp.float32,
     )

time: 342 us -> 393 us (1.15)
  starting transfers between devices: 14 us -> 47.3 us
  waiting for transfers between devices: 264 us -> 279 us
    all_to_all x0 -> x1, waiting for transfers between devices: none -> 104 us  [body(): lax.all_to_all(jnp.stack([rounded] * lax.axis_size('ex')), 'ex', 0, 0)]
    all_gather x1 -> x0, waiting for transfers between devices: 88.7 us -> none  [body(): lax.all_gather(rounded, 'ex', axis=0, tiled=True)]
    all_to_all x1, starting transfers between devices: 13.9 us -> 34 us  [body(): lax.all_to_all(products, 'ex', split_axis=0, concat_axis=1, tiled=True)]
    all_to_all x0 -> x1, starting transfers between devices: none -> 13.3 us  [body(): lax.all_to_all(jnp.stack([rounded] * lax.axis_size('ex')), 'ex', 0, 0)]
    unnamed x4 -> x3, waiting for transfers between devices: 80.3 us -> 80.3 us
  transfers between devices with their start and end apart: 4 -> 4, of which waited for: 4 -> 4; matrix products, arithmetic and copies ran while one was open for 3% -> 2% of each run, Pallas kernels for 0% -> 0%
where the time goes in v2:
time: 393 us
  waiting for transfers between devices  279 us (71%)
  starting transfers between devices  47.3 us (12%)
  blocking collectives  28.4 us (7%)
  between operations  13.5 us (3%)
  matrix products  12.6 us (3%)
  local copies, waits for them, and re-layouts  10.6 us (3%)
    all_to_all x1, waiting for transfers between devices, body(): lax.all_to_all(jnp.stack([rounded] * lax.axis_size('ex')), 'ex', 0, 0)  104 us
    psum x1, waiting for transfers between devices, body(): adapted = lax.psum(adapted, 'feat')  83.7 us
    unnamed x3, waiting for transfers between devices  80.3 us
    all_to_all x1, starting transfers between devices, body(): lax.all_to_all(products, 'ex', split_axis=0, concat_axis=1, tiled=True)  34 us
    psum x1, blocking collectives, body(): lax.psum((products, valid_squares, train_squares), 'feat')  28.4 us
    all_to_all x1, starting transfers between devices, body(): lax.all_to_all(jnp.stack([rounded] * lax.axis_size('ex')), 'ex', 0, 0)  13.3 us
    all_to_all x1, waiting for transfers between devices, body(): lax.all_to_all(products, 'ex', split_axis=0, concat_axis=1, tiled=True)  11.7 us
  transfers between devices with their start and end apart: 4, of which 4 were waited for; matrix products, arithmetic and copies ran while one was open for 2% of the time, Pallas kernels for 0%

profile of v2, /device:TPU:1, one launch (start us, length us, event | category | flops | bytes accessed | tf_op | source)
XLA Modules:
  0.0 392.9 jit_solution(16814512929769145363)
XLA Ops:
  6.5 0.0 copy-start
  6.5 0.0 copy-start.1
  6.5 0.0 all-reduce.3.cloned.1.call-start
  6.5 2.5 fusion.3
  9.1 0.0 all-reduce.3.cloned.1.call-update
  9.1 0.0 reduce-scatter.4.cloned.1.call-start
  9.1 0.0 copy-done
  9.2 0.0 copy-done.1
  9.2 2.7 fusion.7
  11.9 3.5 copy.21
  15.4 0.0 copy-start.4
  15.4 0.0 copy-start.3
  15.4 0.0 reduce-scatter.4.cloned.1.call-update
  15.5 0.6 copy-done.4
  16.1 0.1 fusion.5
  16.2 83.7 %all-reduce.3.cloned.1.call-done = f32[2,32,24,128]{3,2,1,0:T(8,128)} async-done(((f32[2,32,24,128]{3,2,1,0:T(8,128)}), f32[2,32,24,128]{3,2,1,0:T(8,128)}) %all-reduce.3.cloned.1.call-update) | async-done | bytes 786448 | tf_op jit(solution)/shard_map/psum | solution.py:22
  99.8 0.0 copy-done.3
  99.8 3.2 fusion
  103.0 80.2 %reduce-scatter.4.cloned.1.call-done = f32[64,1536]{1,0:T(8,128)} async-done(((f32[512,1536]{1,0:T(8,128)}), f32[64,1536]{1,0:T(8,128)}) %reduce-scatter.4.cloned.1.call-update) | async-done | bytes 393232
  183.2 1.3 copy.22
  184.5 0.8 multiply_reduce_fusion
  185.3 0.3 copy.16
  185.6 0.1 copy.17
  185.7 2.5 stack.2
  188.2 0.0 copy-start.2
  188.2 13.3 %all-to-all-start = ((bf16[64,32,1024]{2,1,0:T(8,128)(2,1)}), bf16[64,32,1024]{2,1,0:T(8,128)(2,1)}, u32[]{:S(2)}, u32[]{:S(2)}) async-start(bf16[64,32,1024]{2,1,0:T(8,128)(2,1)} %stack.2), calls=%async_computation | async-start | bytes 8388608 | tf_op jit(solution)/shard_map/all_to_all | solution.py:49
  201.5 0.0 copy-done.2
  201.5 0.1 multiply_reduce_fusion.1
  201.7 103.8 %all-to-all-done = bf16[64,32,1024]{2,1,0:T(8,128)(2,1)} async-done(((bf16[64,32,1024]{2,1,0:T(8,128)(2,1)}), bf16[64,32,1024]{2,1,0:T(8,128)(2,1)}, u32[]{:S(2)}, u32[]{:S(2)}) %all-to-all-start) | async-done | bytes 4194336 | tf_op jit(solution)/shard_map/all_to_all | solution.py:49
  305.5 3.4 fusion.8
  308.8 28.4 %all-reduce = (f32[2048,4]{0,1:T(4,128)S(1)}, f32[4]{0:T(128)S(1)}, f32[32]{0:T(128)S(1)}) all-reduce(f32[2048,4]{0,1:T(4,128)S(1)} %fusion.8, f32[4]{0:T(128)S(1)} %multiply_reduce_fusion.1, f32[32]{0:T(128)S(1)} %get-tuple-element.8), channel_id=1, replica_groups=mesh['ex'=64,'feat'=8] {'feat'}, use_global_device_ids=true, to_apply=%region_2.0 | all-reduce | flops 8228 | bytes 65824 | tf_op jit(solution)/shard_map/psum | solution.py:54
  337.2 0.1 broadcast_divide_fusion.1
  337.3 0.1 all_to_all.14
  337.4 0.1 copy.30
  337.5 0.8 reshape.55
  338.2 34.0 %all-to-all-start.1 = ((f32[64,1,128]{2,1,0:T(1,128)}), f32[64,1,128]{2,1,0:T(1,128)S(1)}, u32[]{:S(2)}, u32[]{:S(2)}) async-start(f32[64,1,128]{2,1,0:T(1,128)} %reshape.55), calls=%async_computation.1 | async-start | bytes 65536 | tf_op jit(solution)/shard_map/all_to_all | solution.py:58
  372.2 11.7 %all-to-all-done.1 = f32[64,1,128]{2,1,0:T(1,128)S(1)} async-done(((f32[64,1,128]{2,1,0:T(1,128)}), f32[64,1,128]{2,1,0:T(1,128)S(1)}, u32[]{:S(2)}, u32[]{:S(2)}) %all-to-all-start.1) | async-done | bytes 32800 | tf_op jit(solution)/shard_map/all_to_all | solution.py:58
  383.9 0.5 broadcast.26
  384.4 0.7 reduce.1
  385.2 0.1 reshape.56
  385.4 0.7 copy.19
  (4 shorter events, 0.1 us)
Async XLA Ops:
  6.5 2.6 copy-start
  6.5 2.6 copy-start.1
  6.5 93.3 %all-reduce.3.cloned.1.call-start = ((), (), s32[]{:S(2)}) async-start(), calls=%async_computation.3 | async-start | bytes 1572864 | tf_op jit(solution)/shard_map/psum | solution.py:22
  9.1 174.1 %reduce-scatter.4.cloned.1.call-start = ((), (), s32[]{:S(2)}) async-start(), calls=%async_computation.4 | async-start | bytes 3538944
  15.4 0.7 copy-start.4
  15.4 84.4 %copy-start.3 = (bf16[2,128,16]{1,2,0:T(8,128)(2,1)S(1)}, bf16[2,128,16]{1,2,0:T(8,128)(2,1)}, u32[]{:S(2)}) copy-start(bf16[2,128,16]{1,2,0:T(8,128)(2,1)} %param.12) | copy-start | bytes 24580
  188.2 13.3 %copy-start.2 = (bf16[4,1024]{1,0:T(4,128)(2,1)S(1)}, bf16[4,1024]{1,0:T(4,128)(2,1)}, u32[]{:S(2)}) copy-start(bf16[4,1024]{1,0:T(4,128)(2,1)} %param.13) | copy-start | bytes 24580
  188.2 117.3 %all-to-all-start = ((bf16[64,32,1024]{2,1,0:T(8,128)(2,1)}), bf16[64,32,1024]{2,1,0:T(8,128)(2,1)}, u32[]{:S(2)}, u32[]{:S(2)}) async-start(bf16[64,32,1024]{2,1,0:T(8,128)(2,1)} %stack.2), calls=%async_computation | async-start | bytes 8388608 | tf_op jit(solution)/shard_map/all_to_all | solution.py:49
  338.2 45.7 %all-to-all-start.1 = ((f32[64,1,128]{2,1,0:T(1,128)}), f32[64,1,128]{2,1,0:T(1,128)S(1)}, u32[]{:S(2)}, u32[]{:S(2)}) async-start(f32[64,1,128]{2,1,0:T(1,128)} %reshape.55), calls=%async_computation.1 | async-start | bytes 65536 | tf_op jit(solution)/shard_map/all_to_all | solution.py:58
Sparse Core Ops, SparseCore 0:
  10.3 89.4 all-reduce.2
  102.7 80.5 reduce-scatter.3
